TPU v7x, 128 devices: a whole 4x4x4 slice. The times are simulated.
128 devices in a mesh: feat: 8 (over x, z_lo), seq: 16 (over z_hi, y, core).
Axes of the slice: x: 4, y: 4, z: 4 (z_hi: 2, z_lo: 2; z = z_hi * 2 + z_lo), core: 2. Of those that a mesh axis runs over, the one named last changes fastest.
Arguments:
- tokens: bfloat16 [8192, 8192], P('seq', 'feat'), may hold values from -6 to 6
- block_weights: bfloat16 [28672, 512], P('feat'), may hold values from -0.25 to 0.25
- left_factor: bfloat16 [28672, 256], P('feat'), may hold values from -0.09375 to 0.09375
- right_factor: bfloat16 [8192, 256], P('feat'), may hold values from -0.0625 to 0.0625
- pattern: int32 [224, 4], P('feat'), may hold values from 0 to 63, as said below
- cotangent: bfloat16 [8192, 28672], P('seq', 'feat'), may hold values from -6 to 6
Outputs:
- activated: bfloat16 [8192, 28672], P('seq', 'feat')
- grad_input: bfloat16 [16, 512, 8192], P('seq', 'feat')
- grad_blocks: float32 [28672, 512], P(('feat', 'seq'))
- grad_left: float32 [28672, 256], P(('feat', 'seq'))
- grad_right: float32 [8192, 256], P(('feat', 'seq'))
Inputs may be any that keep to these rules, and one draw needn't show every extreme that they name: For block row f, pattern[f, 0] // 8 equals (f * 8) // 224, and pattern[f, j] = pattern[f, 0] XOR ((64) >> j) for 1 <= j < 4.
All inputs are finite; a program needn't handle non-finite values.
Results may differ from a plain program's by a relative error of at most 0.0051.
Values may be sent and summed in bfloat16 or wider, within the bound.
A program may use at most 192 MiB of HBM per device.

v0:
```python
import math
import jax
import jax.numpy as jnp
from jax import lax
from jax.sharding import PartitionSpec as P

BLK = 128
LEVELS = 4


def from_partner(value, axis, distance):
    mask = 2**distance
    pairs = [(source, source ^ mask) for source in range(lax.axis_size(axis))]
    return lax.ppermute(value, axis, pairs)


def activation(values):
    return jax.nn.gelu(values, approximate=True)


def partner_bit(stride, local_blocks):
    return (stride // local_blocks).bit_length() - 1


def local(tokens, block_weights, left_factor, right_factor, pattern, cotangent):
    tok_rows, local_width = tokens.shape
    feat_count = lax.axis_size("feat")
    seq_count = lax.axis_size("seq")
    norm_scale = 1.0 / math.sqrt(tok_rows * seq_count)
    local_blocks = local_width // BLK
    all_blocks = local_blocks * feat_count
    row_blocks = pattern.shape[0]
    out_rows = block_weights.shape[0]
    weight_blocks = block_weights.reshape(row_blocks, BLK, LEVELS, BLK)
    strides = [0] + [all_blocks >> level for level in range(1, LEVELS)]
    pieces = []
    for level in range(LEVELS):
        bit_index = partner_bit(strides[level], local_blocks) if level > 0 else -1
        source = tokens if bit_index < 0 else from_partner(tokens, "feat", bit_index)
        local_ids = pattern[:, level] % local_blocks
        pieces.append(jnp.take(source.reshape(tok_rows, local_blocks, BLK), local_ids, axis=1))
    picked = jnp.stack(pieces, axis=2)
    sparse = jnp.einsum("tfli,foli->tfo", picked, weight_blocks, preferred_element_type=jnp.float32)
    latent_part = jnp.dot(tokens, right_factor, preferred_element_type=jnp.float32)
    latent = lax.psum(latent_part, "feat").astype(jnp.bfloat16)
    pre = sparse.reshape(tok_rows, out_rows) + jnp.einsum(
        "tr,or->to", latent, left_factor, preferred_element_type=jnp.float32
    )
    activated, slope = jax.vjp(activation, pre)
    grad_pre = slope(cotangent.astype(jnp.float32))[0].astype(jnp.bfloat16)
    back_part = jnp.einsum("to,or->tr", grad_pre, left_factor, preferred_element_type=jnp.float32)
    back_latent = lax.psum(back_part, "feat").astype(jnp.bfloat16)
    low_rank = jnp.einsum(
        "tr,ir->ti", back_latent, right_factor, preferred_element_type=jnp.float32
    )
    grad_rows = grad_pre.reshape(tok_rows, row_blocks, BLK)
    spread = jnp.einsum(
        "tfo,foli->tfli", grad_rows, weight_blocks, preferred_element_type=jnp.float32
    )
    summed_grad = low_rank
    for level in range(LEVELS):
        bit_index = partner_bit(strides[level], local_blocks) if level > 0 else -1
        local_ids = pattern[:, level] % local_blocks
        level_term = (
            jnp.zeros((tok_rows, local_blocks, BLK), jnp.float32)
            .at[:, local_ids, :]
            .add(spread[:, :, level, :])
        )
        level_term = level_term.reshape(tok_rows, local_width)
        if bit_index >= 0:
            level_term = from_partner(level_term, "feat", bit_index)
        summed_grad = summed_grad + level_term
    local_grad = summed_grad.astype(jnp.bfloat16)
    regrouped = lax.all_to_all(local_grad, "feat", split_axis=0, concat_axis=1, tiled=True)
    grad_input = regrouped.reshape(1, tok_rows // feat_count, feat_count * local_width)
    window = min(out_rows // seq_count * lax.axis_size("seq") // BLK + 2, row_blocks)
    product = jnp.einsum("tfo,tfli->foli", grad_rows, picked, preferred_element_type=jnp.float32)
    product = product.reshape(window * BLK, LEVELS * BLK) * norm_scale
    grad_blocks = lax.psum_scatter(product, "seq", scatter_dimension=0, tiled=True)
    left_term = (
        jnp.einsum("to,tr->or", grad_pre, latent, preferred_element_type=jnp.float32) * norm_scale
    )
    right_term = (
        jnp.einsum("ti,tr->ir", tokens, back_latent, preferred_element_type=jnp.float32)
        * norm_scale
    )
    grad_left, grad_right = (
        lax.psum_scatter(left_term, "seq", scatter_dimension=0, tiled=True),
        lax.psum_scatter(right_term, "seq", scatter_dimension=0, tiled=True),
    )
    return (activated.astype(jnp.bfloat16), grad_input, grad_blocks, grad_left, grad_right)


def solution(mesh):
    in_specs = (
        P("seq", "feat"),
        P("feat", None),
        P("feat", None),
        P("feat", None),
        P("feat", None),
        P("seq", "feat"),
    )
    out_specs = (
        P("seq", "feat"),
        P("seq", "feat", None),
        P(("feat", "seq"), None),
        P(("feat", "seq"), None),
        P(("feat", "seq"), None),
    )
    return jax.shard_map(local, mesh=mesh, in_specs=in_specs, out_specs=out_specs, check_vma=False)
```

profile of v0, /device:TPU:0, one launch (start us, length us, event | category | flops | bytes accessed | tf_op | source)
XLA Modules:
  0.0 451.5 jit_solution(5003942331406243700)
XLA Ops:
  13.1 2.7 collective-permute-start
  19.3 6.3 %reshape.62 = bf16[28,128,4,128]{3,2,1,0:T(4,128)(2,1)} reshape(bf16[3584,512]{1,0:T(8,128)(2,1)} %param.9) | data formatting | bytes 7340032 | tf_op jit(solution)/shard_map/reshape | solution.py:34
  25.7 2.9 gather_fusion
  28.5 61.9 %all-reduce.2 = bf16[512,256]{1,0:T(8,128)(2,1)} all-reduce(f32[512,256]{1,0:T(8,128)S(1)} %fusion.36), channel_id=1, replica_groups=mesh['feat'=8,'seq'=16] {'feat'}, use_global_device_ids=true, to_apply=%region_0.2 | all-reduce | flops 131072 | bytes 786432 | tf_op jit(solution)/shard_map/psum | solution.py:45
  96.6 2.9 gather_fusion.2
  99.5 4.2 gather_fusion.3
  103.7 2.9 gather_fusion.1
  106.6 5.8 %select_bitcast_fusion = (bf16[512,28,1,128]{3,0,2,1:T(8,128)(2,1)S(1)}, bf16[512,28,1,128]{3,0,2,1:T(8,128)(2,1)}) fusion(bf16[28,512,128]{2,1,0:T(8,128)(2,1)} %gather_fusion.3, pred[28]{0:T(512)(128)(4,1)S(1)} %get-tuple-element.46, bf16[28,512,128]{2,1,0:T(8,128)(2,1)} %gather_fusion.2, pred[28]{0:T(512)(128)(4,1)S(1)} %get-tuple-element.48), kind=kLoop, calls=%fused_computation.32 | loop fusion | flops 3670016 | bytes 14680120 | tf_op jit(solution)/shard_map/stack | solution.py:42
  112.6 4.1 select_bitcast_fusion.2
  117.3 9.7 %fusion.11 = f32[28,512,128,1]{1,2,3,0:T(8,128)} fusion(bf16[28,128,4,128]{3,2,1,0:T(4,128)(2,1)S(1)} %copy-done.5, bf16[512,28,1,128]{3,0,2,1:T(8,128)(2,1)S(1)} %get-tuple-element.50, bf16[512,28,1,128]{3,0,2,1:T(8,128)(2,1)} %get-tuple-element.51, bf16[512,28,1,128]{3,0,2,1:T(8,128)(2,1)} %get-tuple-element.52, ...), kind=kOutput, calls=%fused_computation.38 | convolution fusion | flops 1901068288 | bytes 25690112 | tf_op jit(solution)/shard_map/tfli,foli->tfo/dot_general | solution.py:43
  127.0 8.5 %copy.63 = f32[512,3584]{1,0:T(8,128)} copy(f32[512,3584]{0,1:T(8,128)} %bitcast.128) | data formatting | bytes 14680064 | tf_op jit(solution)/shard_map/reshape | solution.py:46
  135.5 10.3 %fusion.2 = (bf16[512,3584]{1,0:T(8,128)(2,1)S(1)}, bf16[512,3584]{1,0:T(8,128)(2,1)}) fusion(bf16[512,3584]{1,0:T(8,128)(2,1)} %param.13, f32[512,3584]{1,0:T(8,128)} %copy.63, bf16[512,256]{1,0:T(8,128)(2,1)S(1)} %copy-done.10, bf16[3584,256]{1,0:T(8,128)(2,1)S(1)} %copy-done), kind=kOutput, calls=%fused_computation.16 | convolution fusion | flops 983564288 | bytes 20447232 | tf_op jit(solution)/shard_map/tr,or->to/dot_general | solution.py:46
  149.6 40.0 %all-reduce.3 = bf16[512,256]{1,0:T(8,128)(2,1)S(1)} all-reduce(f32[512,256]{1,0:T(8,128)} %fusion.37), channel_id=1, replica_groups=mesh['feat'=8,'seq'=16] {'feat'}, use_global_device_ids=true, to_apply=%region_1.3 | all-reduce | flops 131072 | bytes 786432 | tf_op jit(solution)/shard_map/psum | solution.py:52
  191.4 5.0 %convolution_multiply_fusion = f32[3584,256]{1,0:T(8,128)} fusion(bf16[512,3584]{1,0:T(8,128)(2,1)} %copy-done.7, bf16[512,256]{1,0:T(8,128)(2,1)S(1)} %copy-done.10), kind=kOutput, calls=%fused_computation.31 | convolution fusion | flops 940441600 | bytes 7602176 | tf_op jit(solution)/shard_map/to,tr->or/dot_general | solution.py:81
  196.5 6.0 %copy.64 = bf16[512,3584]{0,1:T(8,128)(2,1)} copy(bf16[512,3584]{1,0:T(8,128)(2,1)} %copy-done.7) | data formatting | bytes 7340032 | tf_op jit(solution)/shard_map/convert_element_type | solution.py:50
  202.5 10.9 %broadcast_multiply_fusion = f32[28,128,4,128]{3,1,2,0:T(8,128)} fusion(bf16[512,28,128,1]{0,2,3,1:T(8,128)(2,1)} %bitcast.126, bf16[512,28,1,128]{3,0,2,1:T(8,128)(2,1)} %copy-done.8, bf16[512,28,1,128]{3,0,2,1:T(8,128)(2,1)} %get-tuple-element.51, bf16[512,28,1,128]{3,0,2,1:T(8,128)(2,1)} %get-tuple-element.52, ...), kind=kOutput, calls=%fused_computation.36 | convolution fusion | flops 1939603456 | bytes 25690112 | tf_op jit(solution)/shard_map/tfo,tfli->foli/dot_general | solution.py:77
  213.4 9.2 %copy.72 = f32[28,128,4,128]{3,2,1,0:T(4,128)S(1)} copy(f32[28,128,4,128]{3,1,2,0:T(8,128)} %broadcast_multiply_fusion) | data formatting | bytes 14680064 | tf_op jit(solution)/shard_map/mul | solution.py:78
  222.6 3.8 copy.95
  226.4 17.0 %convolution_bitcast_fusion = f32[512,28,4,128]{3,0,2,1:T(8,128)} fusion(bf16[512,28,128,1]{0,2,3,1:T(8,128)(2,1)} %bitcast.127, bf16[28,128,4,128]{3,2,1,0:T(4,128)(2,1)} %reshape.62), kind=kOutput, calls=%fused_computation.9 | convolution fusion | flops 1879048192 | bytes 36700160 | tf_op jit(solution)/shard_map/tfo,foli->tfli/dot_general | solution.py:57
  243.4 20.2 %slice_bitcast_fusion.3 = (f32[28,512,128]{2,1,0:T(8,128)}, f32[28,512,128]{2,1,0:T(8,128)}, f32[28,512,128]{2,1,0:T(8,128)}, f32[28,512,128]{2,1,0:T(8,128)}) fusion(f32[512,28,4,128]{3,0,2,1:T(8,128)} %convolution_bitcast_fusion), kind=kLoop, calls=%fused_computation.28 | loop fusion | bytes 58720256 | tf_op jit(solution)/shard_map/squeeze | solution.py:67
  265.1 18.0 %scatter_fusion.1 = f32[512,8,128]{2,0,1:T(8,128)} fusion(f32[512,8,128]{2,0,1:T(8,128)} %broadcast.93.clone.2, s32[28]{0:T(128)S(1)} %get-tuple-element.41, f32[28,512,128]{2,1,0:T(8,128)} %get-tuple-element.37), kind=kCustom, calls=%fused_computation.5 | custom fusion | flops 1835008 | bytes 22020208 | tf_op jit(solution)/shard_map/scatter-add | solution.py:67
  283.2 3.3 copy_bitcast_fusion.3
  287.9 17.7 %scatter_fusion.2 = f32[512,8,128]{2,0,1:T(8,128)} fusion(f32[512,8,128]{2,0,1:T(8,128)} %broadcast.93.clone.1, s32[28]{0:T(128)S(1)} %get-tuple-element.42, f32[28,512,128]{2,1,0:T(8,128)} %get-tuple-element.36), kind=kCustom, calls=%fused_computation.6 | custom fusion | flops 1835008 | bytes 22020208 | tf_op jit(solution)/shard_map/scatter-add | solution.py:67
  305.6 3.2 copy_bitcast_fusion.2
  311.3 17.8 %scatter_fusion.3 = f32[512,8,128]{2,0,1:T(8,128)} fusion(f32[512,8,128]{2,0,1:T(8,128)} %broadcast.93.clone, s32[28]{0:T(128)S(1)} %get-tuple-element.43, f32[28,512,128]{2,1,0:T(8,128)} %get-tuple-element.35), kind=kCustom, calls=%fused_computation.7 | custom fusion | flops 1835008 | bytes 22020208 | tf_op jit(solution)/shard_map/scatter-add | solution.py:67
  329.1 3.2 copy_bitcast_fusion.1
  335.3 17.7 %scatter_fusion = f32[512,8,128]{2,0,1:T(8,128)} fusion(f32[512,8,128]{2,0,1:T(8,128)} %broadcast.93.clone.3, s32[28]{0:T(128)S(1)} %get-tuple-element.40, f32[28,512,128]{2,1,0:T(8,128)} %get-tuple-element.34), kind=kCustom, calls=%fused_computation.4 | custom fusion | flops 1835008 | bytes 22020208 | tf_op jit(solution)/shard_map/scatter-add | solution.py:67
  353.0 12.0 %collective-permute-done.4 = f32[512,1024]{1,0:T(8,128)} collective-permute-done((f32[512,1024]{1,0:T(8,128)}, f32[512,1024]{1,0:T(8,128)}, u32[]{:S(2)}, u32[]{:S(2)}) %collective-permute-start.4) | collective-permute-done | bytes 2097184 | tf_op jit(solution)/shard_map/ppermute | solution.py:14
  365.0 9.2 %collective-permute-done.5 = f32[512,1024]{1,0:T(8,128)} collective-permute-done((f32[512,1024]{1,0:T(8,128)}, f32[512,1024]{1,0:T(8,128)}, u32[]{:S(2)}, u32[]{:S(2)}) %collective-permute-start.5) | collective-permute-done | bytes 2097184 | tf_op jit(solution)/shard_map/ppermute | solution.py:14
  374.2 4.2 fusion.16
  378.4 15.6 %all_to_all.16 = bf16[8,64,1024]{2,1,0:T(8,128)(2,1)S(1)} all-to-all(bf16[8,64,1024]{2,1,0:T(8,128)(2,1)S(1)} %bitcast.129), channel_id=1, replica_groups=mesh['feat'=8,'seq'=16] {'feat'}, dimensions={0} | all-to-all | bytes 2097152 | tf_op jit(solution)/shard_map/all_to_all | solution.py:74
  395.9 49.1 %reduce-scatter.6.cloned.1.call-done = f32[224,512]{1,0:T(8,128)} async-done(((f32[3584,512]{1,0:T(8,128)}), f32[224,512]{1,0:T(8,128)}) %reduce-scatter.6.cloned.1.call-update) | async-done | bytes 458768 | tf_op jit(solution)/shard_map/reduce_scatter | solution.py:79
  (62 shorter events, 32.4 us)
Async XLA Ops:
  7.2 128.3 %copy-start = (bf16[3584,256]{1,0:T(8,128)(2,1)S(1)}, bf16[3584,256]{1,0:T(8,128)(2,1)}, u32[]{:S(2)}) copy-start(bf16[3584,256]{1,0:T(8,128)(2,1)} %param.10) | copy-start | bytes 5505028
  7.2 10.5 %copy-start.11 = (s32[28,4]{0,1:T(4,128)S(1)}, s32[28,4]{0,1:T(4,128)}, u32[]{:S(2)}) copy-start(s32[28,4]{0,1:T(4,128)} %param.12) | copy-start | bytes 1348
  7.2 388.7 %reduce-scatter.10.cloned.1.call-start = ((), (), s32[]{:S(2)}) async-start(), calls=%async_computation.6 | async-start | bytes 1114112
  9.6 80.8 %collective-permute-start.1 = (bf16[512,1024]{0,1:T(8,128)(2,1)}, bf16[512,1024]{0,1:T(8,128)(2,1)}, u32[]{:S(2)}, u32[]{:S(2)}) collective-permute-start(bf16[512,1024]{0,1:T(8,128)(2,1)} %copy.54), channel_id=1, source_target_pairs={{0,32},{16,48},{32,0},{48,16},{64,96},{80,112},{96,64},{112,80},{1... | collective-permute-start | bytes 3145736 | tf_op jit(solution)/shard_map/ppermute | solution.py:14
  11.2 80.9 %collective-permute-start.2 = (bf16[512,1024]{0,1:T(8,128)(2,1)}, bf16[512,1024]{0,1:T(8,128)(2,1)}, u32[]{:S(2)}, u32[]{:S(2)}) collective-permute-start(bf16[512,1024]{0,1:T(8,128)(2,1)} %copy.54), channel_id=1, source_target_pairs={{0,16},{16,0},{32,48},{48,32},{64,80},{80,64},{96,112},{112,96},{1... | collective-permute-start | bytes 3145736 | tf_op jit(solution)/shard_map/ppermute | solution.py:14
  13.1 81.2 %collective-permute-start = (bf16[512,1024]{0,1:T(8,128)(2,1)}, bf16[512,1024]{0,1:T(8,128)(2,1)}, u32[]{:S(2)}, u32[]{:S(2)}) collective-permute-start(bf16[512,1024]{0,1:T(8,128)(2,1)} %copy.54), channel_id=1, source_target_pairs={{0,64},{16,80},{32,96},{48,112},{64,0},{80,16},{96,32},{112,48},{1... | collective-permute-start | bytes 3145736 | tf_op jit(solution)/shard_map/ppermute | solution.py:14
  99.5 4.2 copy-start.2
  106.6 5.8 %copy-start.3 = (bf16[28,512,128]{2,1,0:T(8,128)(2,1)S(1)}, bf16[28,512,128]{2,1,0:T(8,128)(2,1)}, u32[]{:S(2)}) copy-start(bf16[28,512,128]{2,1,0:T(8,128)(2,1)} %gather_fusion) | copy-start | bytes 11010052
  106.6 6.0 %copy-start.4 = (bf16[28,512,128]{2,1,0:T(8,128)(2,1)S(1)}, bf16[28,512,128]{2,1,0:T(8,128)(2,1)}, u32[]{:S(2)}) copy-start(bf16[28,512,128]{2,1,0:T(8,128)(2,1)} %gather_fusion.1) | copy-start | bytes 11010052
  112.4 4.9 %copy-start.8 = (bf16[512,28,1,128]{3,0,2,1:T(8,128)(2,1)}, bf16[512,28,1,128]{3,0,2,1:T(8,128)(2,1)S(1)}, u32[]{:S(2)}) copy-start(bf16[512,28,1,128]{3,0,2,1:T(8,128)(2,1)S(1)} %get-tuple-element.50) | copy-start | bytes 11010052
  112.6 4.7 %copy-start.5 = (bf16[28,128,4,128]{3,2,1,0:T(4,128)(2,1)S(1)}, bf16[28,128,4,128]{3,2,1,0:T(4,128)(2,1)}, u32[]{:S(2)}) copy-start(bf16[28,128,4,128]{3,2,1,0:T(4,128)(2,1)} %reshape.62) | copy-start | bytes 11010052
  127.0 8.5 %copy-start.10 = (bf16[512,256]{1,0:T(8,128)(2,1)S(1)}, bf16[512,256]{1,0:T(8,128)(2,1)}, u32[]{:S(2)}) copy-start(bf16[512,256]{1,0:T(8,128)(2,1)} %all-reduce.2) | copy-start | bytes 786436
  145.8 1.8 copy-start.7
  147.7 41.9 %copy-start.6 = (bf16[512,1024]{1,0:T(8,128)(2,1)S(1)}, bf16[512,1024]{1,0:T(8,128)(2,1)}, u32[]{:S(2)}) copy-start(bf16[512,1024]{1,0:T(8,128)(2,1)} %param.8) | copy-start | bytes 3145732
  191.3 204.6 %reduce-scatter.8.cloned.1.call-start = ((), (), s32[]{:S(2)}) async-start(), calls=%async_computation.5 | async-start | bytes 3899392 | tf_op jit(solution)/shard_map/reduce_scatter | solution.py:88
  196.4 248.6 %reduce-scatter.6.cloned.1.call-start = ((), (), s32[]{:S(2)}) async-start(), calls=%async_computation.4 | async-start | bytes 7798784 | tf_op jit(solution)/shard_map/reduce_scatter | solution.py:79
  286.4 66.6 %collective-permute-start.3 = (f32[512,1024]{1,0:T(8,128)}, f32[512,1024]{1,0:T(8,128)}, u32[]{:S(2)}, u32[]{:S(2)}) collective-permute-start(f32[512,1024]{1,0:T(8,128)} %copy_bitcast_fusion.3), channel_id=1, source_target_pairs={{0,64},{16,80},{32,96},{48,112},{64,0},{80,16},{96,32},{112,48},{1... | collective-permute-start | bytes 6291464 | tf_op jit(solution)/shard_map/ppermute | solution.py:14
  308.8 56.3 %collective-permute-start.4 = (f32[512,1024]{1,0:T(8,128)}, f32[512,1024]{1,0:T(8,128)}, u32[]{:S(2)}, u32[]{:S(2)}) collective-permute-start(f32[512,1024]{1,0:T(8,128)} %copy_bitcast_fusion.2), channel_id=1, source_target_pairs={{0,32},{16,48},{32,0},{48,16},{64,96},{80,112},{96,64},{112,80},{1... | collective-permute-start | bytes 6291464 | tf_op jit(solution)/shard_map/ppermute | solution.py:14
  332.3 41.9 %collective-permute-start.5 = (f32[512,1024]{1,0:T(8,128)}, f32[512,1024]{1,0:T(8,128)}, u32[]{:S(2)}, u32[]{:S(2)}) collective-permute-start(f32[512,1024]{1,0:T(8,128)} %copy_bitcast_fusion.1), channel_id=1, source_target_pairs={{0,16},{16,0},{32,48},{48,32},{64,80},{80,64},{96,112},{112,96},{1... | collective-permute-start | bytes 6291464 | tf_op jit(solution)/shard_map/ppermute | solution.py:14
  335.3 38.9 %copy-start.9 = (bf16[1024,256]{1,0:T(8,128)(2,1)S(1)}, bf16[1024,256]{1,0:T(8,128)(2,1)}, u32[]{:S(2)}) copy-start(bf16[1024,256]{1,0:T(8,128)(2,1)} %param.11) | copy-start | bytes 1572868
  374.2 70.8 %copy-start.1 = (bf16[3584,256]{1,0:T(8,128)(2,1)S(1)}, bf16[3584,256]{1,0:T(8,128)(2,1)}, u32[]{:S(2)}) copy-start(bf16[3584,256]{1,0:T(8,128)(2,1)} %param.10) | copy-start | bytes 5505028
Sparse Core Ops, SparseCore 0:
  191.4 66.7 reduce-scatter.9
  263.4 77.6 reduce-scatter.7
  346.5 98.4 reduce-scatter.5
where the time goes:
time: 453 us; the launch traced here: 452 us
  blocking collectives  117 us (26%)
  local copies, waits for them, and re-layouts  98.5 us (22%)
  other arithmetic  81.2 us (18%)
  waiting for transfers between devices  70.4 us (16%)
  matrix products  61.3 us (14%)
  between operations  13.9 us (3%)
  starting transfers between devices  8.89 us (2%)
    scatter-add x4, other arithmetic, local(): level_term = jnp.zeros((tok_rows, local_blocks, BLK), jnp.float32).at[:,...  71.2 us
    psum x1, blocking collectives, local(): latent = lax.psum(latent_part, 'feat').astype(jnp.bfloat16)  61.9 us
    reduce_scatter x1, waiting for transfers between devices, local(): lax.psum_scatter(product, 'seq', scatter_dimension=0, tiled=True)  49.1 us
    psum x1, blocking collectives, local(): back_latent = lax.psum(back_part, 'feat').astype(jnp.bfloat16)  40 us
    ppermute x6, waiting for transfers between devices, from_partner(): return lax.ppermute(value, axis, pairs)  21.2 us
    squeeze x1, local copies, waits for them, and re-layouts, local(): spread[:, :, level, :]  20.2 us
    dot_general x1, matrix products, local(): jnp.einsum('tfo,foli->tfli', grad_rows, weight_blocks, preferred_element_...  17 us
    all_to_all x1, blocking collectives, local(): lax.all_to_all(local_grad, 'feat', split_axis=0, concat_axis=1, tiled=True)  15.6 us
  transfers between devices with their start and end apart: 9, of which 3 were waited for; matrix products, arithmetic and copies ran while one was open for 40% of the time, Pallas kernels for 0%

commit v1 on v0

--- a/solution.py
+++ b/solution.py
@@ -49,7 +49,7 @@
     activated, slope = jax.vjp(activation, pre)
     grad_pre = slope(cotangent.astype(jnp.float32))[0].astype(jnp.bfloat16)
     back_part = jnp.einsum("to,or->tr", grad_pre, left_factor, preferred_element_type=jnp.float32)
-    back_latent = lax.psum(back_part, "feat").astype(jnp.bfloat16)
+    back_latent = jnp.sum(lax.all_gather(back_part, "feat"), axis=0).astype(jnp.bfloat16)
     low_rank = jnp.einsum(
         "tr,ir->ti", back_latent, right_factor, preferred_element_type=jnp.float32
     )

time: 453 us -> 476 us (1.051)
  waiting for transfers between devices: 70.4 us -> 125 us
  blocking collectives: 117 us -> 79.9 us
    all_gather x0 -> x1, waiting for transfers between devices: none -> 92.5 us  [local(): lax.all_gather(back_part, 'feat')]
    reduce_scatter x1, waiting for transfers between devices: 49.1 us -> 0.01 us  [local(): lax.psum_scatter(product, 'seq', scatter_dimension=0, tiled=True)]
    psum x1 -> x0, blocking collectives: 40 us -> none  [local(): back_latent = lax.psum(back_part, 'feat').astype(jnp.bfloat16)]
    ppermute x6, waiting for transfers between devices: 21.2 us -> 32.3 us  [from_partner(): return lax.ppermute(value, axis, pairs)]
  transfers between devices with their start and end apart: 9 -> 10, of which waited for: 3 -> 3; matrix products, arithmetic and copies ran while one was open for 40% -> 39% of each run, Pallas kernels for 0% -> 0%
where the time goes in v1:
time: 476 us; the launch traced here: 475 us
  waiting for transfers between devices  125 us (26%)
  local copies, waits for them, and re-layouts  98.5 us (21%)
  other arithmetic  84.4 us (18%)
  blocking collectives  79.9 us (17%)
  matrix products  60.9 us (13%)
  between operations  15.8 us (3%)
  starting transfers between devices  10.2 us (2%)
    all_gather x1, waiting for transfers between devices, local(): lax.all_gather(back_part, 'feat')  92.5 us
    scatter-add x4, other arithmetic, local(): level_term = jnp.zeros((tok_rows, local_blocks, BLK), jnp.float32).at[:,...  71.9 us
    psum x1, blocking collectives, local(): latent = lax.psum(latent_part, 'feat').astype(jnp.bfloat16)  61.9 us
    ppermute x6, waiting for transfers between devices, from_partner(): return lax.ppermute(value, axis, pairs)  32.3 us
    squeeze x1, local copies, waits for them, and re-layouts, local(): spread[:, :, level, :]  20.2 us
    all_to_all x1, blocking collectives, local(): lax.all_to_all(local_grad, 'feat', split_axis=0, concat_axis=1, tiled=True)  18 us
    dot_general x1, matrix products, local(): jnp.einsum('tfo,foli->tfli', grad_rows, weight_blocks, preferred_element_...  17 us
    gather x4, local copies, waits for them, and re-layouts, local(): jnp.take(source.reshape(tok_rows, local_blocks, BLK), local_ids, axis=1)  12.8 us
  transfers between devices with their start and end apart: 10, of which 3 were waited for; matrix products, arithmetic and copies ran while one was open for 39% of the time, Pallas kernels for 0%

profile of v1, /device:TPU:0, one launch (start us, length us, event | category | flops | bytes accessed | tf_op | source)
XLA Modules:
  0.0 474.6 jit_solution(8639758018211684514)
XLA Ops:
  14.0 2.7 collective-permute-start
  20.2 6.3 %reshape.62 = bf16[28,128,4,128]{3,2,1,0:T(4,128)(2,1)} reshape(bf16[3584,512]{1,0:T(8,128)(2,1)} %param.9) | data formatting | bytes 7340032 | tf_op jit(solution)/shard_map/reshape | solution.py:34
  26.5 2.9 gather_fusion
  29.4 61.9 %all-reduce.1 = bf16[512,256]{1,0:T(8,128)(2,1)} all-reduce(f32[512,256]{1,0:T(8,128)S(1)} %fusion.36), channel_id=1, replica_groups=mesh['feat'=8,'seq'=16] {'feat'}, use_global_device_ids=true, to_apply=%region_0.2 | all-reduce | flops 131072 | bytes 786432 | tf_op jit(solution)/shard_map/psum | solution.py:45
  97.5 2.9 gather_fusion.2
  100.4 4.2 gather_fusion.3
  104.6 2.9 gather_fusion.1
  107.5 5.8 %select_bitcast_fusion = (bf16[512,28,1,128]{3,0,2,1:T(8,128)(2,1)S(1)}, bf16[512,28,1,128]{3,0,2,1:T(8,128)(2,1)}) fusion(bf16[28,512,128]{2,1,0:T(8,128)(2,1)} %gather_fusion.3, pred[28]{0:T(512)(128)(4,1)S(1)} %get-tuple-element.46, bf16[28,512,128]{2,1,0:T(8,128)(2,1)} %gather_fusion.2, pred[28]{0:T(512)(128)(4,1)S(1)} %get-tuple-element.48), kind=kLoop, calls=%fused_computation.32 | loop fusion | flops 3670016 | bytes 14680120 | tf_op jit(solution)/shard_map/stack | solution.py:42
  113.5 4.1 select_bitcast_fusion.2
  118.2 9.7 %fusion.11 = f32[28,512,128,1]{1,2,3,0:T(8,128)} fusion(bf16[28,128,4,128]{3,2,1,0:T(4,128)(2,1)S(1)} %copy-done.5, bf16[512,28,1,128]{3,0,2,1:T(8,128)(2,1)S(1)} %get-tuple-element.50, bf16[512,28,1,128]{3,0,2,1:T(8,128)(2,1)} %get-tuple-element.51, bf16[512,28,1,128]{3,0,2,1:T(8,128)(2,1)} %get-tuple-element.52, ...), kind=kOutput, calls=%fused_computation.38 | convolution fusion | flops 1901068288 | bytes 25690112 | tf_op jit(solution)/shard_map/tfli,foli->tfo/dot_general | solution.py:43
  127.9 8.5 %copy.63 = f32[512,3584]{1,0:T(8,128)} copy(f32[512,3584]{0,1:T(8,128)} %bitcast.129) | data formatting | bytes 14680064 | tf_op jit(solution)/shard_map/reshape | solution.py:46
  136.4 10.3 %fusion.2 = (bf16[512,3584]{1,0:T(8,128)(2,1)S(1)}, bf16[512,3584]{1,0:T(8,128)(2,1)}) fusion(bf16[512,3584]{1,0:T(8,128)(2,1)} %param.13, f32[512,3584]{1,0:T(8,128)} %copy.63, bf16[512,256]{1,0:T(8,128)(2,1)S(1)} %copy-done.10, bf16[3584,256]{1,0:T(8,128)(2,1)S(1)} %copy-done), kind=kOutput, calls=%fused_computation.16 | convolution fusion | flops 983564288 | bytes 20447232 | tf_op jit(solution)/shard_map/tr,or->to/dot_general | solution.py:46
  150.5 5.0 %convolution_multiply_fusion = f32[3584,256]{1,0:T(8,128)} fusion(bf16[512,3584]{1,0:T(8,128)(2,1)} %copy-done.7, bf16[512,256]{1,0:T(8,128)(2,1)S(1)} %copy-done.10), kind=kOutput, calls=%fused_computation.31 | convolution fusion | flops 940441600 | bytes 7602176 | tf_op jit(solution)/shard_map/to,tr->or/dot_general | solution.py:81
  155.6 6.0 %copy.64 = bf16[512,3584]{0,1:T(8,128)(2,1)} copy(bf16[512,3584]{1,0:T(8,128)(2,1)} %copy-done.7) | data formatting | bytes 7340032 | tf_op jit(solution)/shard_map/convert_element_type | solution.py:50
  161.6 92.5 %all-gather.3.cloned.1.call-done = f32[4096,256]{1,0:T(8,128)} async-done(((f32[512,256]{1,0:T(8,128)}), f32[4096,256]{1,0:T(8,128)}) %all-gather.3.cloned.1.call-update) | async-done | bytes 4194320 | tf_op jit(solution)/shard_map/all_gather | solution.py:52
  258.5 10.4 %broadcast_multiply_fusion = f32[28,128,4,128]{3,1,2,0:T(8,128)} fusion(bf16[512,28,128,1]{0,2,3,1:T(8,128)(2,1)} %bitcast.127, bf16[512,28,1,128]{3,0,2,1:T(8,128)(2,1)} %copy-done.8, bf16[512,28,1,128]{3,0,2,1:T(8,128)(2,1)} %get-tuple-element.51, bf16[512,28,1,128]{3,0,2,1:T(8,128)(2,1)} %get-tuple-element.52, ...), kind=kOutput, calls=%fused_computation.36 | convolution fusion | flops 1939603456 | bytes 25690112 | tf_op jit(solution)/shard_map/tfo,tfli->foli/dot_general | solution.py:77
  268.9 9.2 %copy.72 = f32[28,128,4,128]{3,2,1,0:T(4,128)S(1)} copy(f32[28,128,4,128]{3,1,2,0:T(8,128)} %broadcast_multiply_fusion) | data formatting | bytes 14680064 | tf_op jit(solution)/shard_map/mul | solution.py:78
  278.1 3.8 copy.95
  282.0 17.0 %convolution_bitcast_fusion = f32[512,28,4,128]{3,0,2,1:T(8,128)} fusion(bf16[512,28,128,1]{0,2,3,1:T(8,128)(2,1)} %bitcast.128, bf16[28,128,4,128]{3,2,1,0:T(4,128)(2,1)} %reshape.62), kind=kOutput, calls=%fused_computation.9 | convolution fusion | flops 1879048192 | bytes 36700160 | tf_op jit(solution)/shard_map/tfo,foli->tfli/dot_general | solution.py:57
  299.0 20.2 %slice_bitcast_fusion.3 = (f32[28,512,128]{2,1,0:T(8,128)}, f32[28,512,128]{2,1,0:T(8,128)}, f32[28,512,128]{2,1,0:T(8,128)}, f32[28,512,128]{2,1,0:T(8,128)}) fusion(f32[512,28,4,128]{3,0,2,1:T(8,128)} %convolution_bitcast_fusion), kind=kLoop, calls=%fused_computation.28 | loop fusion | bytes 58720256 | tf_op jit(solution)/shard_map/squeeze | solution.py:67
  320.7 17.5 %scatter_fusion.1 = f32[512,8,128]{2,0,1:T(8,128)} fusion(f32[512,8,128]{2,0,1:T(8,128)} %broadcast.93.clone.2, s32[28]{0:T(128)S(1)} %get-tuple-element.41, f32[28,512,128]{2,1,0:T(8,128)} %get-tuple-element.37), kind=kCustom, calls=%fused_computation.5 | custom fusion | flops 1835008 | bytes 22020208 | tf_op jit(solution)/shard_map/scatter-add | solution.py:67
  338.3 3.2 copy_bitcast_fusion.3
  341.4 3.8 collective-permute-start.3
  346.8 18.5 %scatter_fusion.2 = f32[512,8,128]{2,0,1:T(8,128)} fusion(f32[512,8,128]{2,0,1:T(8,128)} %broadcast.93.clone.1, s32[28]{0:T(128)S(1)} %get-tuple-element.42, f32[28,512,128]{2,1,0:T(8,128)} %get-tuple-element.36), kind=kCustom, calls=%fused_computation.6 | custom fusion | flops 1835008 | bytes 22020208 | tf_op jit(solution)/shard_map/scatter-add | solution.py:67
  365.3 3.2 copy_bitcast_fusion.2
  370.0 17.8 %scatter_fusion.3 = f32[512,8,128]{2,0,1:T(8,128)} fusion(f32[512,8,128]{2,0,1:T(8,128)} %broadcast.93.clone, s32[28]{0:T(128)S(1)} %get-tuple-element.43, f32[28,512,128]{2,1,0:T(8,128)} %get-tuple-element.35), kind=kCustom, calls=%fused_computation.7 | custom fusion | flops 1835008 | bytes 22020208 | tf_op jit(solution)/shard_map/scatter-add | solution.py:67
  387.7 3.2 copy_bitcast_fusion.1
  392.5 18.2 %scatter_fusion = f32[512,8,128]{2,0,1:T(8,128)} fusion(f32[512,8,128]{2,0,1:T(8,128)} %broadcast.93.clone.3, s32[28]{0:T(128)S(1)} %get-tuple-element.40, f32[28,512,128]{2,1,0:T(8,128)} %get-tuple-element.34), kind=kCustom, calls=%fused_computation.4 | custom fusion | flops 1835008 | bytes 22020208 | tf_op jit(solution)/shard_map/scatter-add | solution.py:67
  410.6 24.8 %collective-permute-done.4 = f32[512,1024]{1,0:T(8,128)} collective-permute-done((f32[512,1024]{1,0:T(8,128)}, f32[512,1024]{1,0:T(8,128)}, u32[]{:S(2)}, u32[]{:S(2)}) %collective-permute-start.4) | collective-permute-done | bytes 2097184 | tf_op jit(solution)/shard_map/ppermute | solution.py:14
  435.4 7.5 %collective-permute-done.5 = f32[512,1024]{1,0:T(8,128)} collective-permute-done((f32[512,1024]{1,0:T(8,128)}, f32[512,1024]{1,0:T(8,128)}, u32[]{:S(2)}, u32[]{:S(2)}) %collective-permute-start.5) | collective-permute-done | bytes 2097184 | tf_op jit(solution)/shard_map/ppermute | solution.py:14
  443.0 4.2 fusion.16
  447.2 18.0 %all_to_all.16 = bf16[8,64,1024]{2,1,0:T(8,128)(2,1)S(1)} all-to-all(bf16[8,64,1024]{2,1,0:T(8,128)(2,1)S(1)} %bitcast.130), channel_id=1, replica_groups=mesh['feat'=8,'seq'=16] {'feat'}, dimensions={0} | all-to-all | bytes 2097152 | tf_op jit(solution)/shard_map/all_to_all | solution.py:74
  (65 shorter events, 32.4 us)
Async XLA Ops:
  8.0 128.4 %copy-start = (bf16[3584,256]{1,0:T(8,128)(2,1)S(1)}, bf16[3584,256]{1,0:T(8,128)(2,1)}, u32[]{:S(2)}) copy-start(bf16[3584,256]{1,0:T(8,128)(2,1)} %param.10) | copy-start | bytes 5505028
  8.0 10.5 %copy-start.11 = (s32[28,4]{0,1:T(4,128)S(1)}, s32[28,4]{0,1:T(4,128)}, u32[]{:S(2)}) copy-start(s32[28,4]{0,1:T(4,128)} %param.12) | copy-start | bytes 1348
  8.0 246.1 %all-gather.3.cloned.1.call-start = ((), (), s32[]{:S(2)}) async-start(), calls=%async_computation.6 | async-start | bytes 4718592 | tf_op jit(solution)/shard_map/all_gather | solution.py:52
  10.5 80.8 %collective-permute-start.1 = (bf16[512,1024]{0,1:T(8,128)(2,1)}, bf16[512,1024]{0,1:T(8,128)(2,1)}, u32[]{:S(2)}, u32[]{:S(2)}) collective-permute-start(bf16[512,1024]{0,1:T(8,128)(2,1)} %copy.54), channel_id=1, source_target_pairs={{0,32},{16,48},{32,0},{48,16},{64,96},{80,112},{96,64},{112,80},{1... | collective-permute-start | bytes 3145736 | tf_op jit(solution)/shard_map/ppermute | solution.py:14
  12.0 80.9 %collective-permute-start.2 = (bf16[512,1024]{0,1:T(8,128)(2,1)}, bf16[512,1024]{0,1:T(8,128)(2,1)}, u32[]{:S(2)}, u32[]{:S(2)}) collective-permute-start(bf16[512,1024]{0,1:T(8,128)(2,1)} %copy.54), channel_id=1, source_target_pairs={{0,16},{16,0},{32,48},{48,32},{64,80},{80,64},{96,112},{112,96},{1... | collective-permute-start | bytes 3145736 | tf_op jit(solution)/shard_map/ppermute | solution.py:14
  14.0 81.3 %collective-permute-start = (bf16[512,1024]{0,1:T(8,128)(2,1)}, bf16[512,1024]{0,1:T(8,128)(2,1)}, u32[]{:S(2)}, u32[]{:S(2)}) collective-permute-start(bf16[512,1024]{0,1:T(8,128)(2,1)} %copy.54), channel_id=1, source_target_pairs={{0,64},{16,80},{32,96},{48,112},{64,0},{80,16},{96,32},{112,48},{1... | collective-permute-start | bytes 3145736 | tf_op jit(solution)/shard_map/ppermute | solution.py:14
  100.4 4.2 copy-start.2
  107.5 5.8 %copy-start.3 = (bf16[28,512,128]{2,1,0:T(8,128)(2,1)S(1)}, bf16[28,512,128]{2,1,0:T(8,128)(2,1)}, u32[]{:S(2)}) copy-start(bf16[28,512,128]{2,1,0:T(8,128)(2,1)} %gather_fusion) | copy-start | bytes 11010052
  107.5 6.0 %copy-start.4 = (bf16[28,512,128]{2,1,0:T(8,128)(2,1)S(1)}, bf16[28,512,128]{2,1,0:T(8,128)(2,1)}, u32[]{:S(2)}) copy-start(bf16[28,512,128]{2,1,0:T(8,128)(2,1)} %gather_fusion.1) | copy-start | bytes 11010052
  113.3 4.9 %copy-start.8 = (bf16[512,28,1,128]{3,0,2,1:T(8,128)(2,1)}, bf16[512,28,1,128]{3,0,2,1:T(8,128)(2,1)S(1)}, u32[]{:S(2)}) copy-start(bf16[512,28,1,128]{3,0,2,1:T(8,128)(2,1)S(1)} %get-tuple-element.50) | copy-start | bytes 11010052
  113.5 4.8 %copy-start.5 = (bf16[28,128,4,128]{3,2,1,0:T(4,128)(2,1)S(1)}, bf16[28,128,4,128]{3,2,1,0:T(4,128)(2,1)}, u32[]{:S(2)}) copy-start(bf16[28,128,4,128]{3,2,1,0:T(4,128)(2,1)} %reshape.62) | copy-start | bytes 11010052
  127.9 8.5 %copy-start.10 = (bf16[512,256]{1,0:T(8,128)(2,1)S(1)}, bf16[512,256]{1,0:T(8,128)(2,1)}, u32[]{:S(2)}) copy-start(bf16[512,256]{1,0:T(8,128)(2,1)} %all-reduce.1) | copy-start | bytes 786436
  146.7 1.8 copy-start.7
  150.5 316.6 %reduce-scatter.8.cloned.1.call-start = ((), (), s32[]{:S(2)}) async-start(), calls=%async_computation.5 | async-start | bytes 3899392 | tf_op jit(solution)/shard_map/reduce_scatter | solution.py:88
  155.6 311.4 %reduce-scatter.10.cloned.1.call-start = ((), (), s32[]{:S(2)}) async-start(), calls=%async_computation.7 | async-start | bytes 1114112
  161.6 95.0 %copy-start.6 = (bf16[512,1024]{1,0:T(8,128)(2,1)S(1)}, bf16[512,1024]{1,0:T(8,128)(2,1)}, u32[]{:S(2)}) copy-start(bf16[512,1024]{1,0:T(8,128)(2,1)} %param.8) | copy-start | bytes 3145732
  258.4 208.6 %reduce-scatter.6.cloned.1.call-start = ((), (), s32[]{:S(2)}) async-start(), calls=%async_computation.4 | async-start | bytes 7798784 | tf_op jit(solution)/shard_map/reduce_scatter | solution.py:79
  341.4 69.2 %collective-permute-start.3 = (f32[512,1024]{1,0:T(8,128)}, f32[512,1024]{1,0:T(8,128)}, u32[]{:S(2)}, u32[]{:S(2)}) collective-permute-start(f32[512,1024]{1,0:T(8,128)} %copy_bitcast_fusion.3), channel_id=1, source_target_pairs={{0,64},{16,80},{32,96},{48,112},{64,0},{80,16},{96,32},{112,48},{1... | collective-permute-start | bytes 6291464 | tf_op jit(solution)/shard_map/ppermute | solution.py:14
  368.5 67.0 %collective-permute-start.4 = (f32[512,1024]{1,0:T(8,128)}, f32[512,1024]{1,0:T(8,128)}, u32[]{:S(2)}, u32[]{:S(2)}) collective-permute-start(f32[512,1024]{1,0:T(8,128)} %copy_bitcast_fusion.2), channel_id=1, source_target_pairs={{0,32},{16,48},{32,0},{48,16},{64,96},{80,112},{96,64},{112,80},{1... | collective-permute-start | bytes 6291464 | tf_op jit(solution)/shard_map/ppermute | solution.py:14
  391.0 52.0 %collective-permute-start.5 = (f32[512,1024]{1,0:T(8,128)}, f32[512,1024]{1,0:T(8,128)}, u32[]{:S(2)}, u32[]{:S(2)}) collective-permute-start(f32[512,1024]{1,0:T(8,128)} %copy_bitcast_fusion.1), channel_id=1, source_target_pairs={{0,16},{16,0},{32,48},{48,32},{64,80},{80,64},{96,112},{112,96},{1... | collective-permute-start | bytes 6291464 | tf_op jit(solution)/shard_map/ppermute | solution.py:14
  392.5 50.5 %copy-start.9 = (bf16[1024,256]{1,0:T(8,128)(2,1)S(1)}, bf16[1024,256]{1,0:T(8,128)(2,1)}, u32[]{:S(2)}) copy-start(bf16[1024,256]{1,0:T(8,128)(2,1)} %param.11) | copy-start | bytes 1572868
  443.0 24.1 %copy-start.1 = (bf16[3584,256]{1,0:T(8,128)(2,1)S(1)}, bf16[3584,256]{1,0:T(8,128)(2,1)}, u32[]{:S(2)}) copy-start(bf16[3584,256]{1,0:T(8,128)(2,1)} %param.10) | copy-start | bytes 5505028
Sparse Core Ops, SparseCore 0:
  150.6 103.4 all-gather.2
Sparse Core Ops, SparseCore 1:
  155.7 98.3 reduce-scatter.7
  258.5 69.6 reduce-scatter.9
  333.4 98.0 reduce-scatter.5
